TPU v7x, 32 devices: a whole 2x2x4 slice. The times are simulated.
32 devices in a mesh: row: 8 (over y, x, core), col: 4 (over z).
Axes of the slice: x: 2, y: 2, z: 4, core: 2. Of those that a mesh axis runs over, the one named last changes fastest.
Arguments:
- matrix: float32 [5120, 5120], P('row', 'col'), may hold values from -64 to 64
Outputs:
- iterate: float32 [5120, 5120], P('row', 'col')
- trace_value: float32 [2], replicated
- frobenius: float32 [2], replicated
All inputs are finite; a program needn't handle non-finite values.
Results may differ from a plain program's by a relative error of at most 0.003.
Values may be sent and summed in bfloat16 or wider, within the bound.
A program may use at most 64 MiB of HBM per device.

v0:
```python
import jax
import jax.numpy as jnp
from jax import lax
from jax.sharding import PartitionSpec as P

ITERS = 2
target = 0.0625


def add_columns(portion, left_panel):
    return jnp.dot(left_panel, portion, preferred_element_type=jnp.float32)


def on_device(matrix):
    rounded = matrix.astype(jnp.bfloat16)
    current = rounded.astype(jnp.float32)
    row_ids = lax.axis_index("row") * matrix.shape[0] + lax.broadcasted_iota(
        jnp.int32, matrix.shape, 0
    )
    col_ids = lax.axis_index("col") * matrix.shape[1] + lax.broadcasted_iota(
        jnp.int32, matrix.shape, 1
    )
    on_diagonal = row_ids == col_ids
    traces = []
    norms = []
    for step in range(ITERS):
        row_panel = lax.all_gather(rounded, "col", axis=1, tiled=True)
        if step == 0:
            order_full = row_panel.shape[1]
            squares = lax.psum(jnp.sum(current * current), ("row", "col"))
            scale = target * order_full / (squares + 1e-06)
            root = jnp.sqrt(scale)
        else:
            scale = jnp.float32(1.0)
            root = jnp.float32(1.0)
        product = add_columns(
            lax.all_gather(rounded, "row", axis=0, tiled=True), left_panel=row_panel
        )
        squared = (product * scale).astype(jnp.bfloat16)
        cubic_part = add_columns(
            lax.all_gather(squared, "row", axis=0, tiled=True), left_panel=row_panel
        )
        current = root * (1.5 * current - 0.5 * cubic_part)
        rounded = current.astype(jnp.bfloat16)
        diagonal_part = jnp.sum(jnp.where(on_diagonal, current, 0.0))
        square_part = jnp.sum(current * current)
        trace_now, total_now = lax.psum((diagonal_part, square_part), ("row", "col"))
        traces.append(trace_now)
        norms.append(jnp.sqrt(total_now))
    return (current, jnp.stack(traces), jnp.stack(norms))


def solution(mesh):
    in_specs = (P("row", "col"),)
    out_specs = (P("row", "col"), P(), P())
    return jax.shard_map(
        on_device, mesh=mesh, in_specs=in_specs, out_specs=out_specs, check_vma=False
    )
```

profile of v0, /device:TPU:0, one launch (start us, length us, event | category | flops | bytes accessed | tf_op | source)
XLA Modules:
  0.0 667.8 jit_solution(10903226945213668132)
XLA Ops:
  7.2 0.0 all-gather.7.cloned.1.call-start
  7.2 4.0 copy.4
  11.2 0.0 copy-start
  11.2 0.0 all-gather.7.cloned.1.call-update
  11.2 0.0 all-gather.9.cloned.1.call-start
  11.3 0.7 all-gather.9.cloned.1.call-update
  12.0 0.0 all-gather.11.cloned.1.call-start
  12.0 0.6 copy-done
  12.6 1.4 fusion.4
  14.1 51.2 %psum.35 = f32[]{:T(128)} all-reduce(f32[]{:T(128)} %fusion.4), channel_id=1, replica_groups=mesh['row'=8,'col'=4] {'row','col'}, use_global_device_ids=true, to_apply=%region_1.0 | all-reduce | flops 1 | bytes 8 | tf_op jit(solution)/shard_map/psum | solution.py:30
  65.9 68.8 %all-gather.7.cloned.1.call-done = bf16[640,5120]{0,1:T(8,128)(2,1)} async-done(((bf16[640,1280]{0,1:T(8,128)(2,1)}), bf16[640,5120]{0,1:T(8,128)(2,1)}) %all-gather.7.cloned.1.call-update) | async-done | bytes 6553616 | tf_op jit(solution)/shard_map/all_gather | solution.py:27
  134.8 74.7 %all-gather.9.cloned.1.call-done = bf16[5120,1280]{0,1:T(8,128)(2,1)} async-done(((bf16[640,1280]{0,1:T(8,128)(2,1)}), bf16[5120,1280]{0,1:T(8,128)(2,1)}) %all-gather.9.cloned.1.call-update) | async-done | bytes 13107216 | tf_op jit(solution)/shard_map/all_gather | solution.py:37
  209.4 14.1 %fusion.7 = bf16[640,1280]{1,0:T(8,128)(2,1)} fusion(bf16[640,5120]{0,1:T(8,128)(2,1)} %all-gather.7.cloned.1.call-done, bf16[5120,1280]{0,1:T(8,128)(2,1)} %all-gather.9.cloned.1.call-done, f32[]{:T(128)S(6)} %div.3), kind=kOutput, calls=%fused_computation.16 | convolution fusion | flops 8390246400 | bytes 21299204 | tf_op jit(solution)/shard_map/dot_general | solution.py:11
  223.5 0.0 all-gather.11.cloned.1.call-update
  223.6 0.0 all-gather.13.cloned.1.call-start
  223.7 74.2 %all-gather.11.cloned.1.call-done = bf16[5120,1280]{1,0:T(8,128)(2,1)} async-done(((bf16[640,1280]{1,0:T(8,128)(2,1)}), bf16[5120,1280]{1,0:T(8,128)(2,1)}) %all-gather.11.cloned.1.call-update) | async-done | bytes 13107216 | tf_op jit(solution)/shard_map/all_gather | solution.py:41
  297.9 18.0 %multiply_reduce_fusion.1 = (f32[]{:T(128)}, f32[]{:T(128)}, bf16[640,1280]{0,1:T(8,128)(2,1)}, f32[640,1280]{0,1:T(8,128)}) fusion(s32[1280]{0:T(1024)S(1)} %iota_add_fusion, s32[640]{0:T(1024)S(1)} %iota_add_fusion.1, bf16[5120,1280]{1,0:T(8,128)(2,1)} %all-gather.11.cloned.1.call-done, bf16[640,5120]{0,1:T(8,128)(2,1)} %all-gather.7.cloned.1.call-done, ...), kind=kOutput, calls=%fused_computation.15 | convolution fusion | flops 8397619200 | bytes 26222092 | tf_op jit(solution)/shard_map/dot_general | solution.py:11
  315.9 0.0 all-gather.13.cloned.1.call-update
  316.0 0.0 all-gather.15.cloned.1.call-start
  316.0 0.5 all-gather.15.cloned.1.call-update
  316.6 0.2 all-gather.17.cloned.1.call-start
  316.8 118.9 %all-gather.13.cloned.1.call-done = bf16[640,5120]{0,1:T(8,128)(2,1)} async-done(((bf16[640,1280]{0,1:T(8,128)(2,1)}), bf16[640,5120]{0,1:T(8,128)(2,1)}) %all-gather.13.cloned.1.call-update) | async-done | bytes 6553616 | tf_op jit(solution)/shard_map/all_gather | solution.py:27
  435.7 74.0 %all-gather.15.cloned.1.call-done = bf16[5120,1280]{0,1:T(8,128)(2,1)} async-done(((bf16[640,1280]{0,1:T(8,128)(2,1)}), bf16[5120,1280]{0,1:T(8,128)(2,1)}) %all-gather.15.cloned.1.call-update) | async-done | bytes 13107216 | tf_op jit(solution)/shard_map/all_gather | solution.py:37
  509.7 14.1 %convolution_convert_fusion = bf16[640,1280]{1,0:T(8,128)(2,1)} fusion(bf16[640,5120]{0,1:T(8,128)(2,1)} %all-gather.13.cloned.1.call-done, bf16[5120,1280]{0,1:T(8,128)(2,1)} %all-gather.15.cloned.1.call-done), kind=kOutput, calls=%fused_computation.17 | convolution fusion | flops 8389427200 | bytes 21299200 | tf_op jit(solution)/shard_map/dot_general | solution.py:11
  523.8 0.0 all-gather.17.cloned.1.call-update
  523.8 74.4 %all-gather.17.cloned.1.call-done = bf16[5120,1280]{1,0:T(8,128)(2,1)} async-done(((bf16[640,1280]{1,0:T(8,128)(2,1)}), bf16[5120,1280]{1,0:T(8,128)(2,1)}) %all-gather.17.cloned.1.call-update) | async-done | bytes 13107216 | tf_op jit(solution)/shard_map/all_gather | solution.py:41
  598.2 17.0 %multiply_reduce_fusion = (f32[]{:T(128)}, f32[]{:T(128)}, f32[640,1280]{0,1:T(8,128)S(1)}) fusion(s32[1280]{0:T(1024)S(1)} %iota_add_fusion, s32[640]{0:T(1024)S(1)} %iota_add_fusion.1, bf16[640,5120]{0,1:T(8,128)(2,1)} %all-gather.13.cloned.1.call-done, bf16[5120,1280]{1,0:T(8,128)(2,1)} %all-gather.17.cloned.1.call-done, f32[640,1280]{0,1:T(8,128)} %get-tuple-element.15), kind=kOutput, calls=%fused_computation.14 | convolution fusion | flops 8395161600 | bytes 26222088 | tf_op jit(solution)/shard_map/dot_general | solution.py:11
  615.2 2.9 copy.6
  618.1 39.6 %all-reduce = (f32[1]{0:T(128)}, f32[1]{0:T(128)}, f32[]{:T(128)}, f32[]{:T(128)}) all-reduce(f32[1]{0:T(128)} %bitcast.2, f32[1]{0:T(128)} %bitcast.1, f32[]{:T(128)} %get-tuple-element.8, f32[]{:T(128)} %get-tuple-element.6), channel_id=1, replica_groups=mesh['row'=8,'col'=4] {'row','col'}, use_global_device_ids=true, to_apply=%region_5.6 | all-reduce | flops 4 | bytes 32 | tf_op jit(solution)/shard_map/psum | solution.py:47
  659.1 1.8 pad_maximum_fusion
  (2 shorter events, 0.0 us)
Async XLA Ops:
  7.2 127.6 %all-gather.7.cloned.1.call-start = ((), (), s32[]{:S(2)}) async-start(), calls=%async_computation | async-start | bytes 8192000 | tf_op jit(solution)/shard_map/all_gather | solution.py:27
  11.2 1.4 copy-start
  11.2 198.2 %all-gather.9.cloned.1.call-start = ((), (), s32[]{:S(2)}) async-start(), calls=%async_computation.1 | async-start | bytes 14745600 | tf_op jit(solution)/shard_map/all_gather | solution.py:37
  12.0 286.0 %all-gather.11.cloned.1.call-start = ((), (), s32[]{:S(2)}) async-start(), calls=%async_computation.2 | async-start | bytes 14745600 | tf_op jit(solution)/shard_map/all_gather | solution.py:41
  223.6 212.2 %all-gather.13.cloned.1.call-start = ((), (), s32[]{:S(2)}) async-start(), calls=%async_computation.3 | async-start | bytes 8192000 | tf_op jit(solution)/shard_map/all_gather | solution.py:27
  316.0 193.8 %all-gather.15.cloned.1.call-start = ((), (), s32[]{:S(2)}) async-start(), calls=%async_computation.4 | async-start | bytes 14745600 | tf_op jit(solution)/shard_map/all_gather | solution.py:37
  316.6 281.6 %all-gather.17.cloned.1.call-start = ((), (), s32[]{:S(2)}) async-start(), calls=%async_computation.5 | async-start | bytes 14745600 | tf_op jit(solution)/shard_map/all_gather | solution.py:41
Sparse Core Ops, SparseCore 0:
  11.3 123.3 all-gather.6
  137.2 72.1 all-gather.8
  223.7 74.1 all-gather.10
  316.1 119.5 all-gather.12
  437.5 72.2 all-gather.14
  524.0 74.1 all-gather.16
where the time goes:
time: 668 us
  waiting for transfers between devices  486 us (73%)
  blocking collectives  90.8 us (14%)
  matrix products  63.2 us (9%)
  between operations  16.2 us (2%)
  local copies, waits for them, and re-layouts  7.52 us (1%)
    all_gather x2, waiting for transfers between devices, on_device(): row_panel = lax.all_gather(rounded, 'col', axis=1, tiled=True)  188 us
    all_gather x2, waiting for transfers between devices, on_device(): lax.all_gather(rounded, 'row', axis=0, tiled=True)  149 us
    all_gather x2, waiting for transfers between devices, on_device(): lax.all_gather(squared, 'row', axis=0, tiled=True)  149 us
    dot_general x4, matrix products, add_columns(): return jnp.dot(left_panel, portion, preferred_element_type=jnp.float32)  63.2 us
    psum x1, blocking collectives, on_device(): squares = lax.psum(jnp.sum(current * current), ('row', 'col'))  51.2 us
    psum x1, blocking collectives, on_device(): lax.psum((diagonal_part, square_part), ('row', 'col'))  39.6 us
  transfers between devices with their start and end apart: 6, of which 6 were waited for; matrix products, arithmetic and copies ran while one was open for 0% of the time, Pallas kernels for 0%

commit v1 on v0

--- a/solution.py
+++ b/solution.py
@@ -2,6 +2,7 @@
 import jax.numpy as jnp
 from jax import lax
 from jax.sharding import PartitionSpec as P
+from jax.lax import axis_index, ppermute, psum
 
 ITERS = 2
 target = 0.0625
@@ -24,7 +25,16 @@
     traces = []
     norms = []
     for step in range(ITERS):
-        row_panel = lax.all_gather(rounded, "col", axis=1, tiled=True)
+        k_all = psum(1, "col")
+        base_arr = sorted(((c, (c + 1) % k_all) for c in range(k_all)))
+        prior = rounded
+        all_rows = [prior]
+        for rr in range(1, k_all):
+            prior = ppermute(prior, "col", base_arr)
+            all_rows.insert(0, prior)
+        a_now = jnp.concatenate(all_rows, 1)
+        arr_now = axis_index("col") + 1
+        row_panel = jnp.roll(a_now, arr_now * rounded.shape[1], 1)
         if step == 0:
             order_full = row_panel.shape[1]
             squares = lax.psum(jnp.sum(current * current), ("row", "col"))

time: 668 us -> 568 us (0.85)
  waiting for transfers between devices: 486 us -> 338 us
  other arithmetic: 3.28 us -> 50 us
  local copies, waits for them, and re-layouts: 7.52 us -> 0.01 us
    ppermute x0 -> x6, waiting for transfers between devices: none -> 192 us  [on_device(): prior = ppermute(prior, 'col', base_arr)]
    all_gather x2 -> x0, waiting for transfers between devices: 188 us -> none  [on_device(): row_panel = lax.all_gather(rounded, 'col', axis=1, tiled=True)]
    all_gather x2, waiting for transfers between devices: 149 us -> 0.01 us  [on_device(): lax.all_gather(rounded, 'row', axis=0, tiled=True)]
    concatenate x0 -> x2, other arithmetic: none -> 43.7 us  [on_device(): row_panel = jnp.roll(a_now, arr_now * rounded.shape[1], 1)]
    unnamed x4, local copies, waits for them, and re-layouts: 7.52 us -> 0.01 us
  transfers between devices with their start and end apart: 6 -> 10, of which waited for: 6 -> 7; matrix products, arithmetic and copies ran while one was open for 0% -> 8% of each run, Pallas kernels for 0% -> 0%
where the time goes in v1:
time: 568 us
  waiting for transfers between devices  338 us (60%)
  blocking collectives  97.4 us (17%)
  matrix products  61.6 us (11%)
  other arithmetic  50 us (9%)
  between operations  16 us (3%)
    ppermute x6, waiting for transfers between devices, on_device(): prior = ppermute(prior, 'col', base_arr)  192 us
    all_gather x2, waiting for transfers between devices, on_device(): lax.all_gather(squared, 'row', axis=0, tiled=True)  146 us
    dot_general x4, matrix products, add_columns(): return jnp.dot(left_panel, portion, preferred_element_type=jnp.float32)  61.6 us
    psum x1, blocking collectives, on_device(): squares = lax.psum(jnp.sum(current * current), ('row', 'col'))  57.8 us
    concatenate x2, other arithmetic, on_device(): row_panel = jnp.roll(a_now, arr_now * rounded.shape[1], 1)  43.7 us
    psum x1, blocking collectives, on_device(): lax.psum((diagonal_part, square_part), ('row', 'col'))  39.6 us
  transfers between devices with their start and end apart: 10, of which 7 were waited for; matrix products, arithmetic and copies ran while one was open for 8% of the time, Pallas kernels for 0%

profile of v1, /device:TPU:0, one launch (start us, length us, event | category | flops | bytes accessed | tf_op | source)
XLA Modules:
  0.0 568.0 jit_solution(3937116264766120435)
XLA Ops:
  7.2 0.0 all-gather.5.cloned.1.call-start
  7.2 4.5 fusion.16
  11.7 0.0 all-gather.5.cloned.1.call-update
  11.7 0.0 all-gather.7.cloned.1.call-start
  11.7 3.1 collective-permute-start
  14.8 38.0 %collective-permute-done = bf16[640,1280]{1,0:T(8,128)(2,1)S(1)} collective-permute-done((bf16[640,1280]{1,0:T(8,128)(2,1)}, bf16[640,1280]{1,0:T(8,128)(2,1)S(1)}, u32[]{:S(2)}, u32[]{:S(2)}) %collective-permute-start) | collective-permute-done | bytes 1638432 | tf_op jit(solution)/shard_map/ppermute | solution.py:33
  52.9 0.0 collective-permute-start.1
  52.9 38.8 %collective-permute-done.1 = bf16[640,1280]{1,0:T(8,128)(2,1)S(1)} collective-permute-done((bf16[640,1280]{1,0:T(8,128)(2,1)S(1)}, bf16[640,1280]{1,0:T(8,128)(2,1)S(1)}, u32[]{:S(2)}, u32[]{:S(2)}) %collective-permute-start.1) | collective-permute-done | bytes 1638432 | tf_op jit(solution)/shard_map/ppermute | solution.py:33
  91.6 0.0 collective-permute-start.2
  91.6 57.8 %psum.35 = f32[]{:T(128)} all-reduce(f32[]{:T(128)} %get-tuple-element.12), channel_id=1, replica_groups=mesh['row'=8,'col'=4] {'row','col'}, use_global_device_ids=true, to_apply=%region_1.2 | all-reduce | flops 1 | bytes 8 | tf_op jit(solution)/shard_map/psum | solution.py:40
  150.1 0.0 collective-permute-done.2
  150.1 21.9 %fusion.10 = bf16[640,5120]{1,0:T(8,128)(2,1)} fusion(s32[]{:T(128)S(6)} %select_n.22, bf16[640,1280]{1,0:T(8,128)(2,1)} %collective-permute-done.2, bf16[640,1280]{1,0:T(8,128)(2,1)S(1)} %collective-permute-done.1, bf16[640,1280]{1,0:T(8,128)(2,1)S(1)} %collective-permute-done, bf16[640,1280]{1,0:T(8,128)(2,1)} %get-tuple-element.13), kind=kLoop, calls=%fused_computation.26 | loop fusion | flops 52428800 | bytes 13107204 | tf_op jit(solution)/shard_map/jit(_roll_dynamic)/concatenate | solution.py:37
  172.1 0.0 copy-start
  172.1 0.0 all-gather.5.cloned.1.call-done
  172.1 14.1 %fusion.19 = bf16[640,1280]{1,0:T(8,128)(2,1)} fusion(bf16[640,5120]{1,0:T(8,128)(2,1)} %fusion.10, bf16[5120,1280]{1,0:T(8,128)(2,1)} %all-gather.5.cloned.1.call-done, f32[]{:T(128)S(6)} %div.3), kind=kOutput, calls=%fused_computation.45 | convolution fusion | flops 8390246400 | bytes 21299204 | tf_op jit(solution)/shard_map/dot_general | solution.py:12
  186.2 0.0 all-gather.7.cloned.1.call-update
  186.2 0.2 all-gather.9.cloned.1.call-start
  186.5 74.1 %all-gather.7.cloned.1.call-done = bf16[5120,1280]{1,0:T(8,128)(2,1)} async-done(((bf16[640,1280]{1,0:T(8,128)(2,1)}), bf16[5120,1280]{1,0:T(8,128)(2,1)}) %all-gather.7.cloned.1.call-update) | async-done | bytes 13107216 | tf_op jit(solution)/shard_map/all_gather | solution.py:51
  260.6 0.0 copy-done
  260.6 16.9 %multiply_reduce_fusion.1 = (f32[]{:T(128)}, f32[]{:T(128)}, bf16[640,1280]{1,0:T(8,128)(2,1)}, f32[640,1280]{1,0:T(8,128)}) fusion(s32[1280]{0:T(1024)S(1)} %iota_add_fusion, s32[640]{0:T(1024)S(1)} %iota_add_fusion.1, bf16[640,5120]{1,0:T(8,128)(2,1)} %fusion.10, bf16[5120,1280]{1,0:T(8,128)(2,1)} %all-gather.7.cloned.1.call-done, ...), kind=kOutput, calls=%fused_computation.43 | convolution fusion | flops 8397619200 | bytes 26222092 | tf_op jit(solution)/shard_map/dot_general | solution.py:12
  277.5 0.0 all-gather.9.cloned.1.call-update
  277.5 0.0 all-gather.11.cloned.1.call-start
  277.6 1.5 collective-permute-start.3
  279.1 38.5 %collective-permute-done.3 = bf16[640,1280]{1,0:T(8,128)(2,1)S(1)} collective-permute-done((bf16[640,1280]{1,0:T(8,128)(2,1)}, bf16[640,1280]{1,0:T(8,128)(2,1)S(1)}, u32[]{:S(2)}, u32[]{:S(2)}) %collective-permute-start.3) | collective-permute-done | bytes 1638432 | tf_op jit(solution)/shard_map/ppermute | solution.py:33
  317.6 0.0 collective-permute-start.4
  317.6 38.9 %collective-permute-done.4 = bf16[640,1280]{1,0:T(8,128)(2,1)S(1)} collective-permute-done((bf16[640,1280]{1,0:T(8,128)(2,1)S(1)}, bf16[640,1280]{1,0:T(8,128)(2,1)S(1)}, u32[]{:S(2)}, u32[]{:S(2)}) %collective-permute-start.4) | collective-permute-done | bytes 1638432 | tf_op jit(solution)/shard_map/ppermute | solution.py:33
  356.5 0.0 collective-permute-start.5
  356.5 38.0 %collective-permute-done.5 = bf16[640,1280]{1,0:T(8,128)(2,1)S(1)} collective-permute-done((bf16[640,1280]{1,0:T(8,128)(2,1)S(1)}, bf16[640,1280]{1,0:T(8,128)(2,1)S(1)}, u32[]{:S(2)}, u32[]{:S(2)}) %collective-permute-start.5) | collective-permute-done | bytes 1638432 | tf_op jit(solution)/shard_map/ppermute | solution.py:33
  394.5 21.8 %fusion.3 = bf16[640,5120]{1,0:T(8,128)(2,1)} fusion(s32[]{:T(128)S(6)} %select_n.22, bf16[640,1280]{1,0:T(8,128)(2,1)S(1)} %collective-permute-done.5, bf16[640,1280]{1,0:T(8,128)(2,1)S(1)} %collective-permute-done.4, bf16[640,1280]{1,0:T(8,128)(2,1)S(1)} %collective-permute-done.3, bf16[640,1280]{1,0:T(8,128)(2,1)} %get-tuple-element.14), kind=kLoop, calls=%fused_computation.19 | loop fusion | flops 52428800 | bytes 13107204 | tf_op jit(solution)/shard_map/jit(_roll_dynamic)/concatenate | solution.py:37
  416.3 0.0 copy-start.1
  416.3 0.0 all-gather.9.cloned.1.call-done
  416.3 14.1 %convolution_convert_fusion = bf16[640,1280]{1,0:T(8,128)(2,1)} fusion(bf16[640,5120]{1,0:T(8,128)(2,1)} %fusion.3, bf16[5120,1280]{1,0:T(8,128)(2,1)} %all-gather.9.cloned.1.call-done), kind=kOutput, calls=%fused_computation.46 | convolution fusion | flops 8389427200 | bytes 21299200 | tf_op jit(solution)/shard_map/dot_general | solution.py:12
  430.5 0.0 all-gather.11.cloned.1.call-update
  430.5 71.6 %all-gather.11.cloned.1.call-done = bf16[5120,1280]{1,0:T(8,128)(2,1)} async-done(((bf16[640,1280]{1,0:T(8,128)(2,1)}), bf16[5120,1280]{1,0:T(8,128)(2,1)}) %all-gather.11.cloned.1.call-update) | async-done | bytes 13107216 | tf_op jit(solution)/shard_map/all_gather | solution.py:51
  502.1 0.0 copy-done.1
  502.1 16.5 %multiply_reduce_fusion = (f32[]{:T(128)}, f32[]{:T(128)}, f32[640,1280]{1,0:T(8,128)}) fusion(s32[1280]{0:T(1024)S(1)} %iota_add_fusion, s32[640]{0:T(1024)S(1)} %iota_add_fusion.1, bf16[640,5120]{1,0:T(8,128)(2,1)} %fusion.3, bf16[5120,1280]{1,0:T(8,128)(2,1)} %all-gather.11.cloned.1.call-done, f32[640,1280]{1,0:T(8,128)S(1)} %copy-done.1), kind=kOutput, calls=%fused_computation.42 | convolution fusion | flops 8395161600 | bytes 26222088 | tf_op jit(solution)/shard_map/dot_general | solution.py:12
  518.6 39.6 %all-reduce = (f32[1]{0:T(128)}, f32[1]{0:T(128)}, f32[]{:T(128)}, f32[]{:T(128)}) all-reduce(f32[1]{0:T(128)} %bitcast.1, f32[1]{0:T(128)} %bitcast, f32[]{:T(128)} %get-tuple-element.6, f32[]{:T(128)} %get-tuple-element.4), channel_id=1, replica_groups=mesh['row'=8,'col'=4] {'row','col'}, use_global_device_ids=true, to_apply=%region_5.7 | all-reduce | flops 4 | bytes 32 | tf_op jit(solution)/shard_map/psum | solution.py:57
  559.7 1.8 pad_maximum_fusion
  (2 shorter events, 0.0 us)
Async XLA Ops:
  7.2 164.9 %all-gather.5.cloned.1.call-start = ((), (), s32[]{:S(2)}) async-start(), calls=%async_computation | async-start | bytes 14745600 | tf_op jit(solution)/shard_map/all_gather | solution.py:47
  11.7 248.9 %all-gather.7.cloned.1.call-start = ((), (), s32[]{:S(2)}) async-start(), calls=%async_computation.1 | async-start | bytes 14745600 | tf_op jit(solution)/shard_map/all_gather | solution.py:51
  11.7 41.1 %collective-permute-start = (bf16[640,1280]{1,0:T(8,128)(2,1)}, bf16[640,1280]{1,0:T(8,128)(2,1)S(1)}, u32[]{:S(2)}, u32[]{:S(2)}) collective-permute-start(bf16[640,1280]{1,0:T(8,128)(2,1)} %get-tuple-element.13), channel_id=1, source_target_pairs={{0,1},{1,2},{2,3},{3,0},{4,5},{5,6},{6,7},{7,4},{8,9},{9,10},{10,1... | collective-permute-start | bytes 4915208 | tf_op jit(solution)/shard_map/ppermute | solution.py:33
  52.9 38.8 %collective-permute-start.1 = (bf16[640,1280]{1,0:T(8,128)(2,1)S(1)}, bf16[640,1280]{1,0:T(8,128)(2,1)S(1)}, u32[]{:S(2)}, u32[]{:S(2)}) collective-permute-start(bf16[640,1280]{1,0:T(8,128)(2,1)S(1)} %collective-permute-done), channel_id=1, source_target_pairs={{0,1},{1,2},{2,3},{3,0},{4,5},{5,6},{6,7},{7,4},{8,9},{9,10},{10,1... | collective-permute-start | bytes 4915208 | tf_op jit(solution)/shard_map/ppermute | solution.py:33
  91.6 58.5 %collective-permute-start.2 = (bf16[640,1280]{1,0:T(8,128)(2,1)S(1)}, bf16[640,1280]{1,0:T(8,128)(2,1)}, u32[]{:S(2)}, u32[]{:S(2)}) collective-permute-start(bf16[640,1280]{1,0:T(8,128)(2,1)S(1)} %collective-permute-done.1), channel_id=1, source_target_pairs={{0,1},{1,2},{2,3},{3,0},{4,5},{5,6},{6,7},{7,4},{8,9},{9,10},{10,1... | collective-permute-start | bytes 4915208 | tf_op jit(solution)/shard_map/ppermute | solution.py:33
  172.1 88.5 %copy-start = (bf16[640,1280]{1,0:T(8,128)(2,1)S(1)}, bf16[640,1280]{1,0:T(8,128)(2,1)}, u32[]{:S(2)}) copy-start(bf16[640,1280]{1,0:T(8,128)(2,1)} %get-tuple-element.13) | copy-start | bytes 4915204
  186.2 230.1 %all-gather.9.cloned.1.call-start = ((), (), s32[]{:S(2)}) async-start(), calls=%async_computation.2 | async-start | bytes 14745600 | tf_op jit(solution)/shard_map/all_gather | solution.py:47
  277.5 224.5 %all-gather.11.cloned.1.call-start = ((), (), s32[]{:S(2)}) async-start(), calls=%async_computation.3 | async-start | bytes 14745600 | tf_op jit(solution)/shard_map/all_gather | solution.py:51
  277.6 40.0 %collective-permute-start.3 = (bf16[640,1280]{1,0:T(8,128)(2,1)}, bf16[640,1280]{1,0:T(8,128)(2,1)S(1)}, u32[]{:S(2)}, u32[]{:S(2)}) collective-permute-start(bf16[640,1280]{1,0:T(8,128)(2,1)} %get-tuple-element.14), channel_id=1, source_target_pairs={{0,1},{1,2},{2,3},{3,0},{4,5},{5,6},{6,7},{7,4},{8,9},{9,10},{10,1... | collective-permute-start | bytes 4915208 | tf_op jit(solution)/shard_map/ppermute | solution.py:33
  317.6 38.9 %collective-permute-start.4 = (bf16[640,1280]{1,0:T(8,128)(2,1)S(1)}, bf16[640,1280]{1,0:T(8,128)(2,1)S(1)}, u32[]{:S(2)}, u32[]{:S(2)}) collective-permute-start(bf16[640,1280]{1,0:T(8,128)(2,1)S(1)} %collective-permute-done.3), channel_id=1, source_target_pairs={{0,1},{1,2},{2,3},{3,0},{4,5},{5,6},{6,7},{7,4},{8,9},{9,10},{10,1... | collective-permute-start | bytes 4915208 | tf_op jit(solution)/shard_map/ppermute | solution.py:33
  356.5 38.0 %collective-permute-start.5 = (bf16[640,1280]{1,0:T(8,128)(2,1)S(1)}, bf16[640,1280]{1,0:T(8,128)(2,1)S(1)}, u32[]{:S(2)}, u32[]{:S(2)}) collective-permute-start(bf16[640,1280]{1,0:T(8,128)(2,1)S(1)} %collective-permute-done.4), channel_id=1, source_target_pairs={{0,1},{1,2},{2,3},{3,0},{4,5},{5,6},{6,7},{7,4},{8,9},{9,10},{10,1... | collective-permute-start | bytes 4915208 | tf_op jit(solution)/shard_map/ppermute | solution.py:33
  416.3 85.7 %copy-start.1 = (f32[640,1280]{1,0:T(8,128)S(1)}, f32[640,1280]{1,0:T(8,128)}, u32[]{:S(2)}) copy-start(f32[640,1280]{1,0:T(8,128)} %get-tuple-element.15) | copy-start | bytes 9830404
Sparse Core Ops, SparseCore 0:
  11.8 76.9 all-gather.4
  186.3 74.2 all-gather.6
  277.7 74.1 all-gather.8
  430.6 71.4 all-gather.10
